TPU v7x, 128 devices: a whole 4x4x4 slice. The times are simulated.
128 devices in a mesh: dp: 8 (over z, core), mp: 16 (over x, y).
Axes of the slice: x: 4, y: 4, z: 4, core: 2. Of those that a mesh axis runs over, the one named last changes fastest.
Arguments:
- tokens: bfloat16 [8192, 4096], P('dp', 'mp'), parts along dimension 0, may hold values from -6 to 6
- cotangent: bfloat16 [8192, 4096], P('dp', 'mp'), parts along dimension 0, may hold values from -6 to 6
- offsets: int32 [64], P('dp'), parts along dimension 0, may hold values from 0 to 960, as said below
- w_gate: bfloat16 [4096, 14336], P(None, 'mp'), may hold values from -0.09375 to 0.09375
- w_up: bfloat16 [4096, 14336], P(None, 'mp'), may hold values from -0.09375 to 0.09375
- w_down: bfloat16 [14336, 4096], P('mp'), may hold values from -0.046875 to 0.046875
- feature_proj: bfloat16 [4096, 192], replicated, may hold values from -0.09375 to 0.09375
- hidden_proj: bfloat16 [14336, 192], P('mp'), may hold values from -0.046875 to 0.046875
Outputs:
- input_grad: bfloat16 [4096, 4096], P(('dp', 'mp')), parts along dimension 0
- projected_grads: float32 [3, 64, 64, 64], P(None, 'dp'), parts along dimension 1
There are 8 independent parts, one for each index of `dp`. A program takes and returns all parts, laid end to end along the dimension named above; an argument that names none is the same for every part. Nothing has to cross between parts.
Inputs may be any that keep to these rules, and one draw needn't show every extreme that they name: `offsets`: spans lie inside the batch and may intersect; in every draw some span starts at 0 and some at 960.
All inputs are finite; a program needn't handle non-finite values.
Results may differ from a plain program's by a relative error of at most 0.0049.
Values may be sent and summed in bfloat16 or wider, within the bound.
No kernel may reach another device: no remote copies, remote signals or barrier semaphores. Data moves between devices by JAX's collectives and lax.ppermute only.
A program may use at most 128 MiB of HBM per device.

v0:
```python
import jax
import jax.numpy as jnp
from jax import lax
from jax.sharding import PartitionSpec as P

RANK = 64
SPAN_LEN = 64


def per_device(tokens, cotangent, offsets, w_gate, w_up, w_down, feature_proj, hidden_proj):
    positions = (offsets[:, None] + jnp.arange(SPAN_LEN, dtype=jnp.int32)[None, :]).reshape(-1)
    span_rows = positions.shape[0]
    span_x = jnp.take(lax.all_gather(tokens, "mp", axis=1, tiled=True), positions, axis=0)
    span_g = jnp.take(lax.all_gather(cotangent, "mp", axis=1, tiled=True), positions, axis=0)
    sums = (
        jnp.dot(span_x, w_gate, preferred_element_type=jnp.float32),
        jnp.dot(span_x, w_up, preferred_element_type=jnp.float32),
        jnp.einsum("td,fd->tf", span_g, w_down, preferred_element_type=jnp.float32),
        jnp.dot(span_x, feature_proj, preferred_element_type=jnp.float32),
        jnp.dot(span_g, feature_proj, preferred_element_type=jnp.float32),
    )
    pre_gate, pre_up, grad_hidden, feat_x, feat_g = sums
    sigmoid_gate = jax.nn.sigmoid(pre_gate)
    activated = pre_gate * sigmoid_gate
    hidden = (activated * pre_up).astype(jnp.bfloat16)
    grad_gate = (
        grad_hidden * pre_up * sigmoid_gate * (1.0 + pre_gate * (1.0 - sigmoid_gate))
    ).astype(jnp.bfloat16)
    grad_up = (grad_hidden * activated).astype(jnp.bfloat16)
    span_count = span_rows // SPAN_LEN
    input_grad = lax.psum_scatter(
        jnp.einsum("tf,df->td", grad_gate, w_gate, preferred_element_type=jnp.float32)
        + jnp.einsum("tf,df->td", grad_up, w_up, preferred_element_type=jnp.float32),
        "mp",
        scatter_dimension=0,
        tiled=True,
    ).astype(jnp.bfloat16)
    hid_gate = jnp.dot(grad_gate, hidden_proj[:, :RANK], preferred_element_type=jnp.float32)
    hid_up = jnp.dot(grad_up, hidden_proj[:, RANK : 2 * RANK], preferred_element_type=jnp.float32)
    hid_down = jnp.dot(hidden, hidden_proj[:, 2 * RANK :], preferred_element_type=jnp.float32)
    hid_gate, hid_up, hid_down = lax.psum((hid_gate, hid_up, hid_down), "mp")

    def per_span(left, right):
        return jnp.einsum(
            "slr,slq->srq",
            left.reshape(span_count, SPAN_LEN, RANK),
            right.reshape(span_count, SPAN_LEN, RANK),
            precision=lax.Precision.HIGHEST,
        )

    projected_grads = jnp.stack(
        [
            per_span(feat_x[:, :RANK], hid_gate),
            per_span(feat_x[:, RANK : 2 * RANK], hid_up),
            per_span(hid_down, feat_g[:, 2 * RANK :]),
        ],
        axis=0,
    )
    return (input_grad, projected_grads)


def solution(mesh):
    in_specs = (
        P("dp", "mp"),
        P("dp", "mp"),
        P("dp"),
        P(None, "mp"),
        P(None, "mp"),
        P("mp", None),
        P(),
        P("mp", None),
    )
    out_specs = (P(("dp", "mp"), None), P(None, "dp", None, None))
    return jax.shard_map(
        per_device, mesh=mesh, in_specs=in_specs, out_specs=out_specs, check_vma=False
    )
```

profile of v0, /device:TPU:0, one launch (start us, length us, event | category | flops | bytes accessed | tf_op | source)
XLA Modules:
  0.0 387.4 jit_solution(1904337492347919827)
XLA Ops:
  7.2 0.7 all-gather.5.cloned.1.call-update
  7.9 0.7 all-gather.3.cloned.1.call-update
  8.7 0.7 iota_add_fusion
  9.4 0.1 add.43
  9.5 80.2 %all-gather.5.cloned.1.call-done = bf16[1024,4096]{1,0:T(8,128)(2,1)} async-done(((bf16[1024,256]{1,0:T(8,128)(2,1)}), bf16[1024,4096]{1,0:T(8,128)(2,1)}) %all-gather.5.cloned.1.call-update) | async-done | bytes 8388624 | tf_op jit(solution)/shard_map/all_gather | solution.py:13
  89.7 13.0 %gather_fusion.1 = bf16[512,4096]{1,0:T(8,128)(2,1)} fusion(bf16[1024,4096]{1,0:T(8,128)(2,1)} %all-gather.5.cloned.1.call-done, s32[1024]{0:T(1024)S(1)} %pad_clamp_fusion), kind=kCustom, calls=%fused_computation.1.clone | custom fusion | bytes 8390656 | tf_op jit(solution)/shard_map/jit(_take)/gather | solution.py:13
  102.7 11.0 %fusion.18 = f32[512,896]{1,0:T(8,128)S(1)} fusion(bf16[4096,896]{1,0:T(8,128)(2,1)} %param.14, bf16[512,4096]{1,0:T(8,128)(2,1)} %gather_fusion.1, pred[512]{0:T(512)(128)(4,1)S(1)} %compare_and_fusion), kind=kOutput, calls=%fused_computation.34 | convolution fusion | flops 3760193536 | bytes 13369856 | tf_op jit(solution)/shard_map/dot_general | solution.py:17
  113.8 9.1 %fusion.17 = f32[512,896]{1,0:T(8,128)S(1)} fusion(bf16[4096,896]{1,0:T(8,128)(2,1)} %param.13, bf16[512,4096]{1,0:T(8,128)(2,1)S(1)} %copy-done, pred[512]{0:T(512)(128)(4,1)S(1)} %compare_and_fusion), kind=kOutput, calls=%fused_computation.33 | convolution fusion | flops 3760193536 | bytes 13369856 | tf_op jit(solution)/shard_map/dot_general | solution.py:16
  122.9 1.2 copy-done.3
  124.2 0.7 fusion.3
  124.8 43.5 %all-gather.3.cloned.1.call-done = bf16[1024,4096]{1,0:T(8,128)(2,1)} async-done(((bf16[1024,256]{1,0:T(8,128)(2,1)}), bf16[1024,4096]{1,0:T(8,128)(2,1)}) %all-gather.3.cloned.1.call-update) | async-done | bytes 8388624 | tf_op jit(solution)/shard_map/all_gather | solution.py:14
  168.3 13.2 %gather_fusion = bf16[512,4096]{1,0:T(8,128)(2,1)} fusion(bf16[1024,4096]{1,0:T(8,128)(2,1)} %all-gather.3.cloned.1.call-done, s32[1024]{0:T(1024)S(1)} %pad_clamp_fusion), kind=kCustom, calls=%fused_computation.clone | custom fusion | bytes 8390656 | tf_op jit(solution)/shard_map/jit(_take)/gather | solution.py:14
  181.5 9.8 %multiply_convert_fusion.1 = (bf16[512,896]{1,0:T(8,128)(2,1)S(1)}, bf16[512,896]{1,0:T(8,128)(2,1)S(1)}) fusion(f32[512,896]{1,0:T(8,128)} %copy-done.3, f32[512,896]{1,0:T(8,128)S(1)} %fusion.18, bf16[896,4096]{1,0:T(8,128)(2,1)} %param.15, bf16[512,4096]{1,0:T(8,128)(2,1)} %gather_fusion, pred[512]{0:T(512)(128)(4,1)S(1)} %compare_and_fusion), kind=kOutput, calls=%fused_computation.6 | convolution fusion | flops 3766157312 | bytes 17039872 | tf_op jit(solution)/shard_map/td,fd->tf/dot_general | solution.py:18
  191.4 1.1 fusion.11
  192.5 9.8 %fusion.20 = f32[512,4096]{1,0:T(8,128)} fusion(bf16[512,896]{1,0:T(8,128)(2,1)S(1)} %get-tuple-element.7, bf16[4096,896]{1,0:T(8,128)(2,1)} %param.13), kind=kOutput, calls=%fused_computation.36 | convolution fusion | flops 3758096384 | bytes 16646144 | tf_op jit(solution)/shard_map/tf,df->td/dot_general | solution.py:32
  202.3 1.1 fusion.9
  203.4 0.1 reshape.36
  203.5 0.8 copy.14
  204.3 0.0 reduce-scatter.2.cloned.1.call-start
  204.3 11.3 %convolution_add_fusion = f32[512,4096]{1,0:T(8,128)} fusion(f32[512,4096]{1,0:T(8,128)} %fusion.20, bf16[512,896]{1,0:T(8,128)(2,1)S(1)} %get-tuple-element.6, bf16[4096,896]{1,0:T(8,128)(2,1)} %param.14), kind=kOutput, calls=%fused_computation.2 | convolution fusion | flops 3760193536 | bytes 25034752 | tf_op jit(solution)/shard_map/tf,df->td/dot_general | solution.py:33
  215.6 1.4 copy-done.2
  217.0 3.9 %fusion.16 = f32[512,192]{0,1:T(8,128)S(1)} fusion(bf16[4096,192]{0,1:T(8,128)(2,1)S(1)} %copy-done.2, bf16[512,4096]{1,0:T(8,128)(2,1)} %gather_fusion.1, pred[512]{0:T(512)(128)(4,1)S(1)} %compare_and_fusion), kind=kOutput, calls=%fused_computation.32 | convolution fusion | flops 807403520 | bytes 6160896 | tf_op jit(solution)/shard_map/dot_general | solution.py:19
  221.0 0.1 reshape.32
  221.1 0.1 reshape.34
  221.2 3.5 fusion.1
  224.7 65.8 %all-reduce.3.cloned.1.call-done = (f32[8,64,64]{1,2,0:T(8,128)}, f32[8,64,64]{2,1,0:T(8,128)}, f32[8,64,64]{2,1,0:T(8,128)}) async-done(((f32[8,64,64]{1,2,0:T(8,128)}, f32[8,64,64]{2,1,0:T(8,128)}, f32[8,64,64]{2,1,0:T(8,128)}), (f32[8,64,64]{1,2,0:T(8,128)}, f32[8,64,64]{2,1,0:T(8,128)}, f32[8,64,64]{2,1,0:T(8,128)})) %all-reduce.3.cloned.1.call-update) | async-done | bytes 393232 | tf_op jit(solution)/shard_map/psum | solution.py:41
  290.5 1.3 convolution_bitcast_fusion.2
  291.8 1.4 convolution_bitcast_fusion.1
  293.2 1.3 convolution_bitcast_fusion
  294.5 0.9 pad_maximum_fusion
  295.5 83.6 %reduce-scatter.2.cloned.1.call-done = f32[32,4096]{1,0:T(8,128)} async-done(((f32[512,4096]{1,0:T(8,128)}), f32[32,4096]{1,0:T(8,128)}) %reduce-scatter.2.cloned.1.call-update) | async-done | bytes 524304 | tf_op jit(solution)/shard_map/reduce_scatter | solution.py:31
  379.1 1.8 convert_element_type.14
  (15 shorter events, 0.2 us)
Async XLA Ops:
  7.2 82.5 %all-gather.5.cloned.1.call-start = ((), (), s32[]{:S(2)}) async-start(), calls=%async_computation.2 | async-start | bytes 8912896 | tf_op jit(solution)/shard_map/all_gather | solution.py:13
  7.9 160.4 %all-gather.3.cloned.1.call-start = ((), (), s32[]{:S(2)}) async-start(), calls=%async_computation.1 | async-start | bytes 8912896 | tf_op jit(solution)/shard_map/all_gather | solution.py:14
  8.6 281.8 %all-reduce.3.cloned.1.call-start = ((), (), s32[]{:S(2)}) async-start(), calls=%async_computation.4 | async-start | bytes 1572864 | tf_op jit(solution)/shard_map/psum | solution.py:41
  102.7 11.0 %copy-start = (bf16[512,4096]{1,0:T(8,128)(2,1)S(1)}, bf16[512,4096]{1,0:T(8,128)(2,1)}, u32[]{:S(2)}) copy-start(bf16[512,4096]{1,0:T(8,128)(2,1)} %gather_fusion.1) | copy-start | bytes 12582916
  113.8 10.4 %copy-start.1 = (bf16[896,192]{0,1:T(8,128)(2,1)S(1)}, bf16[896,192]{0,1:T(8,128)(2,1)}, u32[]{:S(2)}) copy-start(bf16[896,192]{0,1:T(8,128)(2,1)} %param.17) | copy-start | bytes 1032196
  122.9 1.3 copy-start.3
  204.3 174.8 %reduce-scatter.2.cloned.1.call-start = ((), (), s32[]{:S(2)}) async-start(), calls=%async_computation.3 | async-start | bytes 8912896 | tf_op jit(solution)/shard_map/reduce_scatter | solution.py:31
  215.6 1.4 copy-start.2
Sparse Core Ops, SparseCore 0:
  10.1 79.5 all-gather.4
  91.8 76.4 all-gather.2
  204.4 86.0 all-reduce.2
  293.8 85.2 reduce-scatter.1
where the time goes:
time: 388 us; the launch traced here: 387 us
  waiting for transfers between devices  274 us (71%)
  matrix products  65.4 us (17%)
  local copies, waits for them, and re-layouts  30.1 us (8%)
  between operations  13.9 us (4%)
    reduce_scatter x1, waiting for transfers between devices, per_device(): lax.psum_scatter(jnp.einsum('tf,df->td', grad_gate, w_gate, preferred_ele...  83.6 us
    all_gather x1, waiting for transfers between devices, per_device(): lax.all_gather(tokens, 'mp', axis=1, tiled=True)  80.2 us
    psum x1, waiting for transfers between devices, per_device(): hid_gate, hid_up, hid_down = lax.psum((hid_gate, hid_up, hid_down), 'mp')  65.8 us
    all_gather x1, waiting for transfers between devices, per_device(): lax.all_gather(cotangent, 'mp', axis=1, tiled=True)  43.5 us
    gather x1, local copies, waits for them, and re-layouts, per_device(): jnp.take(lax.all_gather(cotangent, 'mp', axis=1, tiled=True), positions,...  13.2 us
    gather x1, local copies, waits for them, and re-layouts, per_device(): jnp.take(lax.all_gather(tokens, 'mp', axis=1, tiled=True), positions, axi...  13 us
    dot_general x1, matrix products, per_device(): jnp.einsum('tf,df->td', grad_up, w_up, preferred_element_type=jnp.float32)  11.3 us
    dot_general x1, matrix products, per_device(): jnp.dot(span_x, w_up, preferred_element_type=jnp.float32)  11 us
  transfers between devices with their start and end apart: 4, of which 4 were waited for; matrix products, arithmetic and copies ran while one was open for 15% of the time, Pallas kernels for 0%

commit v1 on v0

--- a/solution.py
+++ b/solution.py
@@ -2,15 +2,20 @@
 import jax.numpy as jnp
 from jax import lax
 from jax.sharding import PartitionSpec as P
+from jax.lax import all_gather
 
 RANK = 64
 SPAN_LEN = 64
 
 
+def push_thing(frame_in, a_name):
+    return jnp.concatenate(all_gather(frame_in, a_name), 1)
+
+
 def per_device(tokens, cotangent, offsets, w_gate, w_up, w_down, feature_proj, hidden_proj):
     positions = (offsets[:, None] + jnp.arange(SPAN_LEN, dtype=jnp.int32)[None, :]).reshape(-1)
     span_rows = positions.shape[0]
-    span_x = jnp.take(lax.all_gather(tokens, "mp", axis=1, tiled=True), positions, axis=0)
+    span_x = jnp.take(push_thing(tokens, "mp"), positions, axis=0)
     span_g = jnp.take(lax.all_gather(cotangent, "mp", axis=1, tiled=True), positions, axis=0)
     sums = (
         jnp.dot(span_x, w_gate, preferred_element_type=jnp.float32),

time: 388 us -> 382 us (0.985)
  waiting for transfers between devices: 274 us -> 261 us
  local copies, waits for them, and re-layouts: 30.1 us -> 37.9 us
    unnamed x8 -> x9, local copies, waits for them, and re-layouts: 2.64 us -> 10.4 us
    all_gather x1, waiting for transfers between devices: 43.5 us -> 36 us  [per_device(): lax.all_gather(cotangent, 'mp', axis=1, tiled=True)]
    all_gather x1, waiting for transfers between devices: 80.2 us -> 73.8 us  [push_thing(): return jnp.concatenate(all_gather(frame_in, a_name), 1)]
  transfers between devices with their start and end apart: 4 -> 4, of which waited for: 4 -> 4; matrix products, arithmetic and copies ran while one was open for 15% -> 17% of each run, Pallas kernels for 0% -> 0%
where the time goes in v1:
time: 382 us; the launch traced here: 381 us
  waiting for transfers between devices  261 us (68%)
  matrix products  65.5 us (17%)
  local copies, waits for them, and re-layouts  37.9 us (10%)
  between operations  13.9 us (4%)
    reduce_scatter x1, waiting for transfers between devices, per_device(): lax.psum_scatter(jnp.einsum('tf,df->td', grad_gate, w_gate, preferred_ele...  83.6 us
    all_gather x1, waiting for transfers between devices, push_thing(): return jnp.concatenate(all_gather(frame_in, a_name), 1)  73.8 us
    psum x1, waiting for transfers between devices, per_device(): hid_gate, hid_up, hid_down = lax.psum((hid_gate, hid_up, hid_down), 'mp')  65.8 us
    all_gather x1, waiting for transfers between devices, per_device(): lax.all_gather(cotangent, 'mp', axis=1, tiled=True)  36 us
    gather x1, local copies, waits for them, and re-layouts, per_device(): jnp.take(lax.all_gather(cotangent, 'mp', axis=1, tiled=True), positions,...  13.2 us
    gather x1, local copies, waits for them, and re-layouts, per_device(): span_x = jnp.take(push_thing(tokens, 'mp'), positions, axis=0)  13.1 us
    dot_general x1, matrix products, per_device(): jnp.einsum('tf,df->td', grad_up, w_up, preferred_element_type=jnp.float32)  11.3 us
    dot_general x1, matrix products, per_device(): jnp.dot(span_x, w_up, preferred_element_type=jnp.float32)  11 us
  transfers between devices with their start and end apart: 4, of which 4 were waited for; matrix products, arithmetic and copies ran while one was open for 17% of the time, Pallas kernels for 0%

profile of v1, /device:TPU:0, one launch (start us, length us, event | category | flops | bytes accessed | tf_op | source)
XLA Modules:
  0.0 381.4 jit_solution(14263999553083885390)
XLA Ops:
  7.2 0.7 all-gather.6.cloned.1.call-update
  7.9 0.7 all-gather.4.cloned.1.call-update
  8.7 0.7 iota_add_fusion
  9.4 0.1 add.43
  9.5 73.8 %all-gather.6.cloned.1.call-done = bf16[16384,256]{1,0:T(8,128)(2,1)} async-done(((bf16[1024,256]{1,0:T(8,128)(2,1)}), bf16[16384,256]{1,0:T(8,128)(2,1)}) %all-gather.6.cloned.1.call-update) | async-done | bytes 8388624 | tf_op jit(solution)/shard_map/all_gather | solution.py:12
  83.3 7.8 %copy.20 = bf16[128,8,16,256]{3,1,2,0:T(8,128)(2,1)} copy(bf16[128,8,16,256]{3,1,0,2:T(8,128)(2,1)} %bitcast.36) | data formatting | bytes 16777216
  91.1 13.1 %gather_fusion.1 = bf16[512,4096]{1,0:T(8,128)(2,1)} fusion(bf16[1024,4096]{1,0:T(8,128)(2,1)} %bitcast.35, s32[1024]{0:T(1024)S(1)} %pad_clamp_fusion), kind=kCustom, calls=%fused_computation.1.clone | custom fusion | bytes 8390656 | tf_op jit(solution)/shard_map/jit(_take)/gather | solution.py:18
  104.1 11.0 %fusion.18 = f32[512,896]{1,0:T(8,128)S(1)} fusion(bf16[4096,896]{1,0:T(8,128)(2,1)} %param.14, bf16[512,4096]{1,0:T(8,128)(2,1)} %gather_fusion.1, pred[512]{0:T(512)(128)(4,1)S(1)} %compare_and_fusion), kind=kOutput, calls=%fused_computation.34 | convolution fusion | flops 3760193536 | bytes 13369856 | tf_op jit(solution)/shard_map/dot_general | solution.py:22
  115.2 9.1 %fusion.17 = f32[512,896]{1,0:T(8,128)S(1)} fusion(bf16[4096,896]{1,0:T(8,128)(2,1)} %param.13, bf16[512,4096]{1,0:T(8,128)(2,1)S(1)} %copy-done, pred[512]{0:T(512)(128)(4,1)S(1)} %compare_and_fusion), kind=kOutput, calls=%fused_computation.33 | convolution fusion | flops 3760193536 | bytes 13369856 | tf_op jit(solution)/shard_map/dot_general | solution.py:21
  124.3 1.3 copy-done.3
  125.6 0.7 fusion.3
  126.3 36.0 %all-gather.4.cloned.1.call-done = bf16[1024,4096]{1,0:T(8,128)(2,1)} async-done(((bf16[1024,256]{1,0:T(8,128)(2,1)}), bf16[1024,4096]{1,0:T(8,128)(2,1)}) %all-gather.4.cloned.1.call-update) | async-done | bytes 8388624 | tf_op jit(solution)/shard_map/all_gather | solution.py:19
  162.2 13.2 %gather_fusion = bf16[512,4096]{1,0:T(8,128)(2,1)} fusion(bf16[1024,4096]{1,0:T(8,128)(2,1)} %all-gather.4.cloned.1.call-done, s32[1024]{0:T(1024)S(1)} %pad_clamp_fusion), kind=kCustom, calls=%fused_computation.clone | custom fusion | bytes 8390656 | tf_op jit(solution)/shard_map/jit(_take)/gather | solution.py:19
  175.4 9.9 %multiply_convert_fusion.1 = (bf16[512,896]{1,0:T(8,128)(2,1)S(1)}, bf16[512,896]{1,0:T(8,128)(2,1)S(1)}) fusion(f32[512,896]{1,0:T(8,128)} %copy-done.3, f32[512,896]{1,0:T(8,128)S(1)} %fusion.18, bf16[896,4096]{1,0:T(8,128)(2,1)} %param.15, bf16[512,4096]{1,0:T(8,128)(2,1)} %gather_fusion, pred[512]{0:T(512)(128)(4,1)S(1)} %compare_and_fusion), kind=kOutput, calls=%fused_computation.6 | convolution fusion | flops 3766157312 | bytes 17039872 | tf_op jit(solution)/shard_map/td,fd->tf/dot_general | solution.py:23
  185.3 1.1 fusion.11
  186.4 9.8 %fusion.20 = f32[512,4096]{1,0:T(8,128)} fusion(bf16[512,896]{1,0:T(8,128)(2,1)S(1)} %get-tuple-element.7, bf16[4096,896]{1,0:T(8,128)(2,1)} %param.13), kind=kOutput, calls=%fused_computation.36 | convolution fusion | flops 3758096384 | bytes 16646144 | tf_op jit(solution)/shard_map/tf,df->td/dot_general | solution.py:37
  196.3 1.1 fusion.9
  197.3 0.1 reshape.44
  197.5 0.8 copy.15
  198.3 11.3 %convolution_add_fusion = f32[512,4096]{1,0:T(8,128)} fusion(f32[512,4096]{1,0:T(8,128)} %fusion.20, bf16[512,896]{1,0:T(8,128)(2,1)S(1)} %get-tuple-element.6, bf16[4096,896]{1,0:T(8,128)(2,1)} %param.14), kind=kOutput, calls=%fused_computation.2 | convolution fusion | flops 3760193536 | bytes 25034752 | tf_op jit(solution)/shard_map/tf,df->td/dot_general | solution.py:38
  209.6 1.4 copy-done.2
  211.0 3.9 %fusion.16 = f32[512,192]{0,1:T(8,128)S(1)} fusion(bf16[4096,192]{0,1:T(8,128)(2,1)S(1)} %copy-done.2, bf16[512,4096]{1,0:T(8,128)(2,1)} %gather_fusion.1, pred[512]{0:T(512)(128)(4,1)S(1)} %compare_and_fusion), kind=kOutput, calls=%fused_computation.32 | convolution fusion | flops 807403520 | bytes 6160896 | tf_op jit(solution)/shard_map/dot_general | solution.py:24
  214.9 0.1 reshape.40
  215.0 0.1 reshape.42
  215.1 3.5 fusion.1
  218.7 65.8 %all-reduce.3.cloned.1.call-done = (f32[8,64,64]{1,2,0:T(8,128)}, f32[8,64,64]{2,1,0:T(8,128)}, f32[8,64,64]{2,1,0:T(8,128)}) async-done(((f32[8,64,64]{1,2,0:T(8,128)}, f32[8,64,64]{2,1,0:T(8,128)}, f32[8,64,64]{2,1,0:T(8,128)}), (f32[8,64,64]{1,2,0:T(8,128)}, f32[8,64,64]{2,1,0:T(8,128)}, f32[8,64,64]{2,1,0:T(8,128)})) %all-reduce.3.cloned.1.call-update) | async-done | bytes 393232 | tf_op jit(solution)/shard_map/psum | solution.py:46
  284.5 1.3 convolution_bitcast_fusion.2
  285.8 1.4 convolution_bitcast_fusion.1
  287.2 1.3 convolution_bitcast_fusion
  288.5 0.9 pad_maximum_fusion
  289.4 83.6 %reduce-scatter.2.cloned.1.call-done = f32[32,4096]{1,0:T(8,128)} async-done(((f32[512,4096]{1,0:T(8,128)}), f32[32,4096]{1,0:T(8,128)}) %reduce-scatter.2.cloned.1.call-update) | async-done | bytes 524304 | tf_op jit(solution)/shard_map/reduce_scatter | solution.py:36
  373.1 1.8 convert_element_type.14
  (16 shorter events, 0.2 us)
Async XLA Ops:
  7.2 76.1 %all-gather.6.cloned.1.call-start = ((), (), s32[]{:S(2)}) async-start(), calls=%async_computation.3 | async-start | bytes 8912896 | tf_op jit(solution)/shard_map/all_gather | solution.py:12
  7.9 154.3 %all-gather.4.cloned.1.call-start = ((), (), s32[]{:S(2)}) async-start(), calls=%async_computation.1 | async-start | bytes 8912896 | tf_op jit(solution)/shard_map/all_gather | solution.py:19
  8.6 275.8 %all-reduce.3.cloned.1.call-start = ((), (), s32[]{:S(2)}) async-start(), calls=%async_computation.4 | async-start | bytes 1572864 | tf_op jit(solution)/shard_map/psum | solution.py:46
  104.1 11.0 %copy-start = (bf16[512,4096]{1,0:T(8,128)(2,1)S(1)}, bf16[512,4096]{1,0:T(8,128)(2,1)}, u32[]{:S(2)}) copy-start(bf16[512,4096]{1,0:T(8,128)(2,1)} %gather_fusion.1) | copy-start | bytes 12582916
  115.2 10.4 %copy-start.1 = (bf16[896,192]{0,1:T(8,128)(2,1)S(1)}, bf16[896,192]{0,1:T(8,128)(2,1)}, u32[]{:S(2)}) copy-start(bf16[896,192]{0,1:T(8,128)(2,1)} %param.17) | copy-start | bytes 1032196
  124.3 1.3 copy-start.3
  198.2 174.8 %reduce-scatter.2.cloned.1.call-start = ((), (), s32[]{:S(2)}) async-start(), calls=%async_computation.2 | async-start | bytes 8912896 | tf_op jit(solution)/shard_map/reduce_scatter | solution.py:36
  209.6 1.4 copy-start.2
Sparse Core Ops, SparseCore 0:
  10.1 73.1 all-gather.5
  85.4 76.7 all-gather.3
  198.3 86.0 all-reduce.2
  287.7 85.2 reduce-scatter.1
